TPU v7x, 32 devices: a whole 2x2x4 slice. The times are simulated.
32 devices in a mesh: dp: 8 (over z, y), grp: 4 (over x, core).
Axes of the slice: x: 2, y: 2, z: 4, core: 2. Of those that a mesh axis runs over, the one named last changes fastest.
Arguments:
- activations: bfloat16 [32, 512, 768], P('dp', None, 'grp'), may hold values from -6 to 6, as said below
- cotangent: bfloat16 [32, 512, 768], P('dp', None, 'grp'), may hold values from -6 to 6
- lengths: int32 [32], P('dp'), may hold values from 64 to 512
- triple_weight: bfloat16 [2, 4, 192, 576], P(None, 'grp'), may hold values from -0.25980762 to 0.25980762, as said below
- triple_bias: float32 [2, 2, 768], P(None, None, 'grp'), may hold values from -1.8 to 1.8, as said below
- output_weight: bfloat16 [2, 768, 768], replicated, may hold values from -1.75 to 1.75
- output_bias: float32 [2, 768], replicated, may hold values from -1.75 to 1.75
- first_gain: float32 [2, 768], replicated, may hold values from 0.25 to 1.75
- first_shift: float32 [2, 768], replicated, may hold values from -1.75 to 1.75
- widen_weight: bfloat16 [2, 4, 192, 768], P(None, 'grp'), may hold values from -0.4375 to 0.4375
- widen_bias: float32 [2, 3072], P(None, 'grp'), may hold values from -1.75 to 1.75
- shrink_weight: bfloat16 [2, 4, 768, 192], P(None, 'grp'), may hold values from -0.21875 to 0.21875
- narrow_bias: float32 [2, 768], P(None, 'grp'), may hold values from -1.75 to 1.75
- second_gain: float32 [2, 768], P(None, 'grp'), may hold values from 0.25 to 1.75
- second_shift: float32 [2, 768], P(None, 'grp'), may hold values from -1.75 to 1.75
Outputs:
- layer_output: bfloat16 [32, 512, 768], P('dp', None, 'grp')
- input_gradient: float32 [32, 512, 768], P('dp', None, 'grp')
- triple_weight_gradient: float32 [2, 4, 192, 576], P(None, 'grp')
- triple_bias_gradient: float32 [2, 2, 768], P(None, None, 'grp')
- output_weight_gradient: float32 [2, 768, 768], replicated
- output_bias_gradient: float32 [2, 768], replicated
- first_gain_gradient: float32 [2, 768], replicated
- first_shift_gradient: float32 [2, 768], replicated
- widen_weight_gradient: float32 [2, 4, 192, 768], P(None, 'grp')
- widen_bias_gradient: float32 [2, 3072], P(None, 'grp')
- narrow_weight_gradient: float32 [2, 4, 768, 192], P(None, 'grp')
- narrow_bias_gradient: float32 [2, 768], P(None, 'grp')
- second_norm_gain_gradient: float32 [2, 768], P(None, 'grp')
- second_shift_gradient: float32 [2, 768], P(None, 'grp')
Inputs may be any that keep to these rules, and one draw needn't show every extreme that they name: `activations`: independent entries of order one. `triple_weight`: independent entries with deviation about 192 ** -0.5. `triple_bias`: independent entries with deviation about 0.3.
All inputs are finite; a program needn't handle non-finite values.
Results may differ from a plain program's by a relative error of at most 0.015.
Values may be sent and summed in bfloat16 or wider, within the bound.
A program may use at most 192 MiB of HBM per device.

v0:
```python
import math
import jax
import jax.numpy as jnp
from jax import lax
from jax.sharding import PartitionSpec as P

HEAD = 64
EPSILON = 1e-05
MASKED = -1e30


def contract_rows(left, right):
    return lax.dot_general(
        left, right, (((0,), (0,)), ((), ())), preferred_element_type=jnp.float32
    )


def contract_cols(left, weight):
    return lax.dot_general(
        left, weight, (((1,), (1,)), ((), ())), preferred_element_type=jnp.float32
    )


def split_heads(block):
    return block.reshape(block.shape[0], block.shape[1] // HEAD, HEAD)


def score_block(queries, keys, length):
    scores = jnp.einsum(
        "qhd,khd->hqk", split_heads(queries), split_heads(keys), preferred_element_type=jnp.float32
    ) * HEAD ** (-0.5)
    visible = jnp.arange(keys.shape[0]) < length
    return jnp.where(visible[None, None, :], scores, MASKED)


def attend_forward(queries, keys, values, lengths):

    def single(inputs):
        query_one, key_one, value_one, length = inputs
        scores = score_block(query_one, key_one, length)
        highest = jnp.max(scores, axis=-1, keepdims=True)
        expon = jnp.exp(scores - highest)
        totals = jnp.sum(expon, axis=-1, keepdims=True)
        weights = (expon / totals).astype(jnp.bfloat16)
        mixed = jnp.einsum(
            "hqk,khd->qhd", weights, split_heads(value_one), preferred_element_type=jnp.float32
        )
        return (mixed.reshape(query_one.shape).astype(jnp.bfloat16), highest, totals)

    return lax.map(single, (queries, keys, values, lengths))


def attend_backward(queries, keys, values, outgrad, highest, totals, lengths):

    def single(inputs):
        query_one, key_one, value_one, grad_one, top, total, length = inputs
        scores = score_block(query_one, key_one, length)
        probs = jnp.exp(scores - top) / total
        weights = probs.astype(jnp.bfloat16)
        grad_heads = split_heads(grad_one)
        grad_probs = jnp.einsum(
            "qhd,khd->hqk", grad_heads, split_heads(value_one), preferred_element_type=jnp.float32
        )
        inner = jnp.sum(probs * grad_probs, axis=-1, keepdims=True)
        grad_scores = (probs * (grad_probs - inner)).astype(jnp.bfloat16)
        factor = HEAD ** (-0.5)
        query_grad = (
            jnp.einsum(
                "hqk,khd->qhd",
                grad_scores,
                split_heads(key_one),
                preferred_element_type=jnp.float32,
            )
            * factor
        )
        key_grad = (
            jnp.einsum(
                "hqk,qhd->khd",
                grad_scores,
                split_heads(query_one),
                preferred_element_type=jnp.float32,
            )
            * factor
        )
        value_grad = jnp.einsum(
            "hqk,qhd->khd", weights, grad_heads, preferred_element_type=jnp.float32
        )
        shape = query_one.shape
        return (
            query_grad.reshape(shape).astype(jnp.bfloat16),
            key_grad.reshape(shape).astype(jnp.bfloat16),
            value_grad.reshape(shape).astype(jnp.bfloat16),
        )

    return lax.map(single, (queries, keys, values, outgrad, highest, totals, lengths))


def gelu_slope(values):
    return 0.5 * (1.0 + lax.erf(values / math.sqrt(2.0))) + values * jnp.exp(
        -0.5 * values * values
    ) / math.sqrt(2.0 * math.pi)


def layer_forward(inputs, lengths, params, layer_params):
    (
        triple_weight,
        triple_bias,
        output_weight,
        output_bias,
        first_gain,
        first_shift,
        widen_weight,
        widen_bias,
        shrink_weight,
        narrow_bias,
        second_gain,
        second_shift,
    ) = params
    group_width = inputs.shape[-1]
    rows = inputs.reshape(-1, group_width)
    projected = jnp.dot(rows, triple_weight[layer_params, 0], preferred_element_type=jnp.float32)
    queries = (
        (projected[:, :group_width] + triple_bias[layer_params, 0])
        .astype(jnp.bfloat16)
        .reshape(inputs.shape)
    )
    keys = projected[:, group_width : 2 * group_width].astype(jnp.bfloat16).reshape(inputs.shape)
    values = (
        (projected[:, 2 * group_width :] + triple_bias[layer_params, 1])
        .astype(jnp.bfloat16)
        .reshape(inputs.shape)
    )
    queries, keys, values, residual = (
        lax.all_to_all(queries, "grp", split_axis=0, concat_axis=2, tiled=True),
        lax.all_to_all(keys, "grp", split_axis=0, concat_axis=2, tiled=True),
        lax.all_to_all(values, "grp", split_axis=0, concat_axis=2, tiled=True),
        lax.all_to_all(inputs, "grp", split_axis=0, concat_axis=2, tiled=True),
    )
    local = queries.shape[0]
    mine = lax.dynamic_slice_in_dim(lengths, lax.axis_index("grp") * local, local)
    attended, highest, totals = attend_forward(queries, keys, values, mine)
    width = attended.shape[-1]
    flat = attended.reshape(-1, width)
    before = (
        residual.reshape(-1, width).astype(jnp.float32)
        + jnp.dot(flat, output_weight[layer_params], preferred_element_type=jnp.float32)
        + output_bias[layer_params]
    )
    center = before - jnp.mean(before, axis=-1, keepdims=True)
    first_inverse = lax.rsqrt(jnp.mean(center * center, axis=-1, keepdims=True) + EPSILON)
    first_normed = center * first_inverse
    hidden = (
        (first_normed * first_gain[layer_params] + first_shift[layer_params])
        .astype(jnp.bfloat16)
        .reshape(attended.shape)
    )
    hidden_group = lax.all_to_all(hidden, "grp", split_axis=2, concat_axis=0, tiled=True)
    group_rows = hidden_group.reshape(-1, group_width)
    widened = (
        jnp.dot(group_rows, widen_weight[layer_params, 0], preferred_element_type=jnp.float32)
        + widen_bias[layer_params]
    )
    gelu_output = jax.nn.gelu(widened, approximate=False).astype(jnp.bfloat16)
    after = (
        group_rows.astype(jnp.float32)
        + jnp.dot(gelu_output, shrink_weight[layer_params, 0], preferred_element_type=jnp.float32)
        + narrow_bias[layer_params]
    )
    row_sum = jnp.sum(after, axis=-1)
    row_square = jnp.sum(after * after, axis=-1)
    total_sum, total_square = lax.psum((row_sum, row_square), "grp")
    average = (total_sum / width)[:, None]
    variance = (total_square / width)[:, None] - average * average
    second_inverse = lax.rsqrt(variance + EPSILON)
    second_normed = (after - average) * second_inverse
    output = (second_normed * second_gain[layer_params] + second_shift[layer_params]).reshape(
        inputs.shape
    )
    kept = (
        inputs,
        queries,
        keys,
        values,
        mine,
        highest,
        totals,
        attended,
        first_normed,
        first_inverse,
        group_rows,
        widened,
        gelu_output,
        second_normed,
        second_inverse,
    )
    return (output, kept)


def layer_backward(outgrad, params, layer_params, kept):
    (
        triple_weight,
        triple_bias,
        output_weight,
        output_bias,
        first_gain,
        first_shift,
        widen_weight,
        widen_bias,
        shrink_weight,
        narrow_bias,
        second_gain,
        second_shift,
    ) = params
    (
        inputs,
        queries,
        keys,
        values,
        mine,
        highest,
        totals,
        attended,
        first_normed,
        first_inverse,
        group_rows,
        widened,
        gelu_output,
        second_normed,
        second_inverse,
    ) = kept
    group_width = inputs.shape[-1]
    width = attended.shape[-1]
    grad_rows = outgrad.reshape(-1, group_width)
    scaled = grad_rows * second_gain[layer_params]
    part_sum = jnp.sum(scaled, axis=-1)
    part_cross = jnp.sum(scaled * second_normed, axis=-1)
    total_sum, total_cross = lax.psum((part_sum, part_cross), "grp")
    grad_after = second_inverse * (
        scaled - (total_sum / width)[:, None] - second_normed * (total_cross / width)[:, None]
    )
    second_gain_grad = jnp.sum(grad_rows * second_normed, axis=0)
    second_shift_grad = jnp.sum(grad_rows, axis=0)
    narrow_rounded = grad_after.astype(jnp.bfloat16)
    narrow_weight_grad = contract_rows(gelu_output, narrow_rounded)
    narrow_bias_grad = jnp.sum(narrow_rounded.astype(jnp.float32), axis=0)
    gelu_output_gradient = contract_cols(narrow_rounded, shrink_weight[layer_params, 0])
    widened_grad = (gelu_output_gradient * gelu_slope(widened)).astype(jnp.bfloat16)
    widen_weight_grad = contract_rows(group_rows, widened_grad)
    widen_bias_grad = jnp.sum(widened_grad.astype(jnp.float32), axis=0)
    hidden_grad = (grad_after + contract_cols(widened_grad, widen_weight[layer_params, 0])).astype(
        jnp.bfloat16
    )
    hidden_seq = lax.all_to_all(
        hidden_grad.reshape(inputs.shape), "grp", split_axis=0, concat_axis=2, tiled=True
    )
    seq_rows = hidden_seq.reshape(-1, width).astype(jnp.float32)
    first_gain_grad = jnp.sum(seq_rows * first_normed, axis=0)
    first_shift_grad = jnp.sum(seq_rows, axis=0)
    scaled_first = seq_rows * first_gain[layer_params]
    grad_before = first_inverse * (
        scaled_first
        - jnp.mean(scaled_first, axis=-1, keepdims=True)
        - first_normed * jnp.mean(scaled_first * first_normed, axis=-1, keepdims=True)
    )
    before_rounded = grad_before.astype(jnp.bfloat16)
    flat = attended.reshape(-1, width)
    output_weight_grad = contract_rows(flat, before_rounded)
    output_bias_grad = jnp.sum(before_rounded.astype(jnp.float32), axis=0)
    attended_grad = (
        contract_cols(before_rounded, output_weight[layer_params])
        .astype(jnp.bfloat16)
        .reshape(attended.shape)
    )
    residual_grad = before_rounded.reshape(attended.shape)
    query_seq, key_seq, value_seq = attend_backward(
        queries, keys, values, attended_grad, highest, totals, mine
    )
    query_grad, key_grad, value_grad, input_part = (
        lax.all_to_all(query_seq, "grp", split_axis=2, concat_axis=0, tiled=True),
        lax.all_to_all(key_seq, "grp", split_axis=2, concat_axis=0, tiled=True),
        lax.all_to_all(value_seq, "grp", split_axis=2, concat_axis=0, tiled=True),
        lax.all_to_all(residual_grad, "grp", split_axis=2, concat_axis=0, tiled=True),
    )
    triple_grad = jnp.concatenate(
        [
            query_grad.reshape(-1, group_width),
            key_grad.reshape(-1, group_width),
            value_grad.reshape(-1, group_width),
        ],
        axis=-1,
    )
    triple_weight_grad = contract_rows(inputs.reshape(-1, group_width), triple_grad)
    triple_bias_grad = jnp.stack(
        [
            jnp.sum(query_grad.reshape(-1, group_width).astype(jnp.float32), axis=0),
            jnp.sum(value_grad.reshape(-1, group_width).astype(jnp.float32), axis=0),
        ]
    )
    input_grad = contract_cols(triple_grad, triple_weight[layer_params, 0]) + input_part.reshape(
        -1, group_width
    ).astype(jnp.float32)
    grads = (
        triple_weight_grad[None],
        triple_bias_grad,
        output_weight_grad,
        output_bias_grad,
        first_gain_grad,
        first_shift_grad,
        widen_weight_grad[None],
        widen_bias_grad,
        narrow_weight_grad[None],
        narrow_bias_grad,
        second_gain_grad,
        second_shift_grad,
    )
    return (input_grad.reshape(inputs.shape), grads)


def shards(
    activations,
    cotangent,
    lengths,
    triple_weight,
    triple_bias,
    output_weight,
    output_bias,
    first_gain,
    first_shift,
    widen_weight,
    widen_bias,
    shrink_weight,
    narrow_bias,
    second_gain,
    second_shift,
):
    params = (
        triple_weight,
        triple_bias,
        output_weight,
        output_bias,
        first_gain,
        first_shift,
        widen_weight,
        widen_bias,
        shrink_weight,
        narrow_bias,
        second_gain,
        second_shift,
    )
    depth = triple_weight.shape[0]
    current = activations
    stored = []
    kept_list = []
    final = None
    for layer_params in range(depth):
        stored.append(current)
        result, kept = layer_forward(current, lengths, params, layer_params)
        kept_list.append(kept)
        final = result
        current = result.astype(jnp.bfloat16)
    outgrad = cotangent.astype(jnp.float32)
    collected = [None] * depth
    for layer_params in reversed(range(depth)):
        replayed, kept = layer_forward(stored[layer_params], lengths, params, layer_params)
        outgrad, layer_param_gradients = layer_backward(outgrad, params, layer_params, kept)
        collected[layer_params] = layer_param_gradients
    stacked = [
        jnp.stack([collected[layer_params][member] for layer_params in range(depth)])
        for member in range(12)
    ]
    group_totals = lax.psum(
        (
            stacked[0],
            stacked[1],
            stacked[6],
            stacked[7],
            stacked[8],
            stacked[9],
            stacked[10],
            stacked[11],
        ),
        "dp",
    )
    shared_totals = lax.psum((stacked[2], stacked[3], stacked[4], stacked[5]), ("dp", "grp"))
    return (
        final.astype(jnp.bfloat16),
        outgrad,
        group_totals[0],
        group_totals[1],
        shared_totals[0],
        shared_totals[1],
        shared_totals[2],
        shared_totals[3],
        group_totals[2],
        group_totals[3],
        group_totals[4],
        group_totals[5],
        group_totals[6],
        group_totals[7],
    )


def solution(mesh):
    in_specs = (
        P("dp", None, "grp"),
        P("dp", None, "grp"),
        P("dp"),
        P(None, "grp", None, None),
        P(None, None, "grp"),
        P(),
        P(),
        P(),
        P(),
        P(None, "grp", None, None),
        P(None, "grp"),
        P(None, "grp", None, None),
        P(None, "grp"),
        P(None, "grp"),
        P(None, "grp"),
    )
    out_specs = (
        P("dp", None, "grp"),
        P("dp", None, "grp"),
        P(None, "grp", None, None),
        P(None, None, "grp"),
        P(),
        P(),
        P(),
        P(),
        P(None, "grp", None, None),
        P(None, "grp"),
        P(None, "grp", None, None),
        P(None, "grp"),
        P(None, "grp"),
        P(None, "grp"),
    )
    return jax.shard_map(shards, mesh=mesh, in_specs=in_specs, out_specs=out_specs, check_vma=False)
```

profile of v0, /device:TPU:0, one launch (start us, length us, event | category | flops | bytes accessed | tf_op | source)
XLA Modules:
  0.0 857.9 jit_solution(8457950099970390052)
XLA Ops:
  31.4 6.9 all-to-all-done.3
  45.1 9.1 %all-to-all-done.2 = bf16[4,512,192]{1,2,0:T(8,128)(2,1)} async-done(((bf16[4,512,192]{1,2,0:T(8,128)(2,1)}), bf16[4,512,192]{1,2,0:T(8,128)(2,1)}, u32[]{:S(2)}, u32[]{:S(2)}) %all-to-all-start.2) | async-done | bytes 786464 | tf_op jit(solution)/shard_map/all_to_all | solution.py:134
  57.7 10.6 %fusion.129 = (f32[12,512]{1,0:T(8,128)S(1)}, f32[12,512,512]{1,2,0:T(8,128)}) fusion(pred[512]{0:T(512)(128)(4,1)S(1)} %iota_compare_fusion, bf16[512,12,64]{0,2,1:T(8,128)(2,1)} %bitcast.12, bf16[512,12,64]{0,2,1:T(8,128)(2,1)S(1)} %bitcast.431), kind=kOutput, calls=%fused_computation.281 | convolution fusion | flops 415236608 | bytes 14180864 | tf_op jit(solution)/shard_map/while/body/eval_jaxpr/sub | solution.py:42
  91.6 10.4 %all-to-all-done.4 = bf16[4,2,49152]{2,1,0:T(2,128)(2,1)S(1)} async-done(((bf16[4,2,49152]{2,1,0:T(2,128)(2,1)}), bf16[4,2,49152]{2,1,0:T(2,128)(2,1)S(1)}, u32[]{:S(2)}, u32[]{:S(2)}) %all-to-all-start.4) | async-done | bytes 786464 | tf_op jit(solution)/shard_map/all_to_all | solution.py:157
  103.8 15.9 %fusion.6 = (bf16[2048,768]{1,0:T(8,128)(2,1)S(1)}, f32[2048,768]{1,0:T(8,128)}) fusion(f32[768]{0:T(1024)S(1)} %get-tuple-element.241, bf16[2048,192]{0,1:T(8,128)(2,1)S(1)} %bitcast.493, bf16[2,1,192,768]{3,2,1,0:T(8,128)(2,1)S(1)} %copy-done.66), kind=kOutput, calls=%fused_computation.18 | convolution fusion | flops 707788800 | bytes 10522624 | tf_op jit(solution)/shard_map/dot_general | solution.py:160
  121.4 10.1 %all-reduce.6 = (f32[2048]{0:T(1024)S(1)}, f32[2048]{0:T(1024)S(1)}) all-reduce(f32[2048]{0:T(1024)S(1)} %get-tuple-element.233, f32[2048]{0:T(1024)S(1)} %get-tuple-element.232), channel_id=1, replica_groups=mesh['dp'=8,'grp'=4] {'grp'}, use_global_device_ids=true, to_apply=%region_7.8 | all-reduce | flops 4096 | bytes 32768 | tf_op jit(solution)/shard_map/psum | solution.py:171
  155.4 8.5 all-to-all-done.8
  171.0 8.9 %all-to-all-done.7 = bf16[4,512,192]{1,2,0:T(8,128)(2,1)} async-done(((bf16[4,512,192]{1,2,0:T(8,128)(2,1)}), bf16[4,512,192]{1,2,0:T(8,128)(2,1)}, u32[]{:S(2)}, u32[]{:S(2)}) %all-to-all-start.7) | async-done | bytes 786464 | tf_op jit(solution)/shard_map/all_to_all | solution.py:134
  183.4 10.5 %fusion.131 = (f32[12,512]{1,0:T(8,128)S(1)}, f32[12,512,512]{1,2,0:T(8,128)}) fusion(pred[512]{0:T(512)(128)(4,1)S(1)} %iota_compare_fusion, bf16[512,12,64]{0,2,1:T(8,128)(2,1)} %bitcast.37, bf16[512,12,64]{0,2,1:T(8,128)(2,1)S(1)} %bitcast.433), kind=kOutput, calls=%fused_computation.283 | convolution fusion | flops 415236608 | bytes 14180864 | tf_op jit(solution)/shard_map/while/body/eval_jaxpr/sub | solution.py:42
  221.9 10.4 %all-to-all-done.9 = bf16[4,2,49152]{2,1,0:T(2,128)(2,1)} async-done(((bf16[4,2,49152]{2,1,0:T(2,128)(2,1)}), bf16[4,2,49152]{2,1,0:T(2,128)(2,1)}, u32[]{:S(2)}, u32[]{:S(2)}) %all-to-all-start.9) | async-done | bytes 786464 | tf_op jit(solution)/shard_map/all_to_all | solution.py:157
  238.5 15.8 %fusion.9 = (bf16[2048,768]{1,0:T(8,128)(2,1)S(1)}, f32[2048,768]{1,0:T(8,128)}) fusion(f32[768]{0:T(1024)S(1)} %get-tuple-element.240, bf16[2048,192]{0,1:T(8,128)(2,1)S(1)} %bitcast.497, bf16[2,1,192,768]{3,2,1,0:T(8,128)(2,1)S(1)} %copy-done.67), kind=kOutput, calls=%fused_computation.21 | convolution fusion | flops 707788800 | bytes 10522624 | tf_op jit(solution)/shard_map/dot_general | solution.py:160
  256.7 10.3 %all-reduce.5 = (f32[2048]{0:T(1024)S(1)}, f32[2048]{0:T(1024)S(1)}) all-reduce(f32[2048]{0:T(1024)S(1)} %get-tuple-element.231, f32[2048]{0:T(1024)S(1)} %get-tuple-element.230), channel_id=1, replica_groups=mesh['dp'=8,'grp'=4] {'grp'}, use_global_device_ids=true, to_apply=%region_15.16 | all-reduce | flops 4096 | bytes 32768 | tf_op jit(solution)/shard_map/psum | solution.py:171
  269.4 10.3 %all-reduce.4 = (f32[2048]{0:T(1024)S(1)}, f32[2048]{0:T(1024)S(1)}) all-reduce(f32[2048]{0:T(1024)S(1)} %get-tuple-element.223, f32[2048]{0:T(1024)S(1)} %bitcast.523), channel_id=1, replica_groups=mesh['dp'=8,'grp'=4] {'grp'}, use_global_device_ids=true, to_apply=%region_19.20 | all-reduce | flops 4096 | bytes 32768 | tf_op jit(solution)/shard_map/psum | solution.py:237
  297.1 11.6 %all-to-all-done.10 = bf16[4,512,192]{1,2,0:T(8,128)(2,1)} async-done(((bf16[4,512,192]{1,2,0:T(8,128)(2,1)}), bf16[4,512,192]{1,2,0:T(8,128)(2,1)}, u32[]{:S(2)}, u32[]{:S(2)}) %all-to-all-start.10) | async-done | bytes 786464 | tf_op jit(solution)/shard_map/all_to_all | solution.py:253
  322.3 6.9 fusion.70
  342.8 11.6 %multiply_reduce_fusion.1 = (f32[12,512]{1,0:T(8,128)S(1)}, f32[12,512,512]{1,2,0:T(8,128)}) fusion(f32[12,512,512]{1,2,0:T(8,128)} %get-tuple-element.302, f32[12,512]{1,0:T(8,128)S(1)} %get-tuple-element.301, bf16[512,12,64]{0,2,1:T(8,128)(2,1)} %bitcast.513, bf16[512,12,64]{0,2,1:T(8,128)(2,1)} %bitcast.510), kind=kOutput, calls=%fused_computation.5 | convolution fusion | flops 412084224 | bytes 26787840 | tf_op jit(solution)/shard_map/while/body/eval_jaxpr/qhd,khd->hqk/dot_general | solution.py:61
  369.7 9.6 %multiply_convert_fusion.1 = bf16[12,512,512]{1,2,0:T(8,128)(2,1)S(1)} fusion(f32[12,512,512]{1,2,0:T(8,128)} %get-tuple-element.309, f32[12,512]{1,0:T(8,128)S(1)} %get-tuple-element.308, f32[12,512,512]{1,2,0:T(8,128)} %get-tuple-element.302, f32[12,512]{1,0:T(8,128)S(1)} %get-tuple-element.301), kind=kLoop, calls=%fused_computation.4 | loop fusion | flops 12582912 | bytes 31506432 | tf_op jit(solution)/shard_map/while/body/eval_jaxpr/convert_element_type | solution.py:65
  440.9 11.9 %all-reduce.3 = (f32[2048]{0:T(1024)S(1)}, f32[2048]{0:T(1024)S(1)}) all-reduce(f32[2048]{0:T(1024)S(1)} %get-tuple-element.221, f32[2048]{0:T(1024)S(1)} %get-tuple-element.228), channel_id=1, replica_groups=mesh['dp'=8,'grp'=4] {'grp'}, use_global_device_ids=true, to_apply=%region_26.27 | all-reduce | flops 4096 | bytes 32768 | tf_op jit(solution)/shard_map/psum | solution.py:237
  495.9 8.9 %multiply_reduce_fusion = (f32[12,512]{1,0:T(8,128)S(1)}, f32[12,512,512]{1,2,0:T(8,128)}) fusion(f32[12,512,512]{1,2,0:T(8,128)} %get-tuple-element.295, f32[12,512]{1,0:T(8,128)S(1)} %copy-done.81, bf16[512,12,64]{0,2,1:T(8,128)(2,1)S(1)} %bitcast.515, bf16[512,12,64]{0,2,1:T(8,128)(2,1)S(1)} %bitcast.508), kind=kOutput, calls=%fused_computation.3 | convolution fusion | flops 412084224 | bytes 26787840 | tf_op jit(solution)/shard_map/while/body/eval_jaxpr/qhd,khd->hqk/dot_general | solution.py:61
  517.2 9.6 %multiply_convert_fusion = bf16[12,512,512]{1,2,0:T(8,128)(2,1)S(1)} fusion(f32[12,512,512]{1,2,0:T(8,128)} %get-tuple-element.312, f32[12,512]{1,0:T(8,128)S(1)} %get-tuple-element.311, f32[12,512,512]{1,2,0:T(8,128)} %get-tuple-element.295, f32[12,512]{1,0:T(8,128)S(1)} %copy-done.81), kind=kLoop, calls=%fused_computation.2 | loop fusion | flops 12582912 | bytes 31506432 | tf_op jit(solution)/shard_map/while/body/eval_jaxpr/convert_element_type | solution.py:65
  558.1 7.5 reduce.35
  614.4 47.1 %all-reduce = (f32[2,768]{1,0:T(2,128)}, f32[2,768]{1,0:T(2,128)}, f32[2,768]{1,0:T(2,128)}) all-reduce(f32[2,768]{1,0:T(2,128)S(1)} %pad_maximum_fusion.4, f32[2,768]{1,0:T(2,128)S(1)} %pad_maximum_fusion.5, f32[2,768]{1,0:T(2,128)S(1)} %pad_maximum_fusion.6), channel_id=1, replica_groups=mesh['dp'=8,'grp'=4] {'dp','grp'}, use_global_device_ids=true, to_apply=%region_39.40 | all-reduce | flops 4608 | bytes 36864 | tf_op jit(solution)/shard_map/psum | solution.py:384
  668.6 37.8 %all-reduce.1 = (f32[2,2,192]{2,1,0:T(2,128)}, f32[2,768]{1,0:T(2,128)}, f32[2,192]{1,0:T(2,128)}, f32[2,192]{1,0:T(2,128)}, f32[2,192]{1,0:T(2,128)}) all-reduce(f32[2,2,192]{2,1,0:T(2,128)S(1)} %pad_maximum_fusion.8, f32[2,768]{1,0:T(2,128)S(1)} %pad_maximum_fusion.7, ...), channel_id=1, replica_groups=mesh['dp'=8,'grp'=4] {'dp'}, use_global_device_ids=true, to_apply=%region_35.36 | all-reduce | flops 3456 | bytes 27648 | tf_op jit(solution)/shard_map/psum | solution.py:371
  706.3 134.4 %all-reduce.12.cloned.1.call-done = (f32[2,1,192,576]{3,2,1,0:T(8,128)}, f32[2,1,192,768]{3,2,1,0:T(8,128)}, f32[2,1,768,192]{2,3,1,0:T(8,128)}) async-done(((f32[2,1,192,576]{3,2,1,0:T(8,128)}, f32[2,1,192,768]{3,2,1,0:T(8,128)}, f32[2,1,768,192]{2,3,1,0:T(8,128)}), (f32[2,1,192,576]{3,2,1,0:T(8,128)}, f32[2,1,192,768]{3,2,1,0:T(8,128)}, f32[2,1,768,192]{2,3,1,0:T(8,128)})) %all-reduce.12.cloned.1.call-update) | async-done | bytes 3244048 | tf_op jit(solution)/shard_map/psum | solution.py:371
  (466 shorter events, 406.7 us)
Async XLA Ops:
  7.2 16.0 %all-to-all-start = ((bf16[4,512,192]{1,2,0:T(8,128)(2,1)}), bf16[4,512,192]{1,2,0:T(8,128)(2,1)S(1)}, u32[]{:S(2)}, u32[]{:S(2)}) async-start(bf16[4,512,192]{1,2,0:T(8,128)(2,1)} %param.15), calls=%async_computation | async-start | bytes 1572864 | tf_op jit(solution)/shard_map/all_to_all | solution.py:137
  23.2 15.1 %all-to-all-start.3 = ((bf16[4,512,192]{1,2,0:T(8,128)(2,1)}), bf16[4,512,192]{1,2,0:T(8,128)(2,1)S(1)}, u32[]{:S(2)}, u32[]{:S(2)}) async-start(bf16[4,512,192]{1,2,0:T(8,128)(2,1)} %bitcast.407), calls=%async_computation.3 | async-start | bytes 1572864 | tf_op jit(solution)/shard_map/all_to_all | solution.py:135
  38.3 15.9 %all-to-all-start.2 = ((bf16[4,512,192]{1,2,0:T(8,128)(2,1)}), bf16[4,512,192]{1,2,0:T(8,128)(2,1)}, u32[]{:S(2)}, u32[]{:S(2)}) async-start(bf16[4,512,192]{1,2,0:T(8,128)(2,1)} %bitcast.408), calls=%async_computation.2 | async-start | bytes 1572864 | tf_op jit(solution)/shard_map/all_to_all | solution.py:134
  54.2 15.1 %all-to-all-start.1 = ((bf16[4,512,192]{1,2,0:T(8,128)(2,1)}), bf16[4,512,192]{1,2,0:T(8,128)(2,1)S(1)}, u32[]{:S(2)}, u32[]{:S(2)}) async-start(bf16[4,512,192]{1,2,0:T(8,128)(2,1)} %bitcast.409), calls=%async_computation.1 | async-start | bytes 1572864 | tf_op jit(solution)/shard_map/all_to_all | solution.py:136
  86.8 15.1 %all-to-all-start.4 = ((bf16[4,2,49152]{2,1,0:T(2,128)(2,1)}), bf16[4,2,49152]{2,1,0:T(2,128)(2,1)S(1)}, u32[]{:S(2)}, u32[]{:S(2)}) async-start(bf16[4,2,49152]{2,1,0:T(2,128)(2,1)} %reshape.507), calls=%async_computation.4 | async-start | bytes 1572864 | tf_op jit(solution)/shard_map/all_to_all | solution.py:157
  91.0 40.6 %copy-start.82 = (f32[1,192]{1,0:T(1,128)}, f32[1,192]{1,0:T(1,128)S(1)}, u32[]{:S(2)}) copy-start(f32[1,192]{1,0:T(1,128)S(1)} %get-tuple-element.289) | copy-start | bytes 2308
  133.5 15.1 %all-to-all-start.5 = ((bf16[4,512,192]{1,2,0:T(8,128)(2,1)}), bf16[4,512,192]{1,2,0:T(8,128)(2,1)S(1)}, u32[]{:S(2)}, u32[]{:S(2)}) async-start(bf16[4,512,192]{1,2,0:T(8,128)(2,1)} %bitcast.406), calls=%async_computation.5 | async-start | bytes 1572864 | tf_op jit(solution)/shard_map/all_to_all | solution.py:137
  148.7 15.3 %all-to-all-start.8 = ((bf16[4,512,192]{1,2,0:T(8,128)(2,1)}), bf16[4,512,192]{1,2,0:T(8,128)(2,1)S(1)}, u32[]{:S(2)}, u32[]{:S(2)}) async-start(bf16[4,512,192]{1,2,0:T(8,128)(2,1)} %bitcast.403), calls=%async_computation.8 | async-start | bytes 1572864 | tf_op jit(solution)/shard_map/all_to_all | solution.py:135
  164.0 15.9 %all-to-all-start.7 = ((bf16[4,512,192]{1,2,0:T(8,128)(2,1)}), bf16[4,512,192]{1,2,0:T(8,128)(2,1)}, u32[]{:S(2)}, u32[]{:S(2)}) async-start(bf16[4,512,192]{1,2,0:T(8,128)(2,1)} %bitcast.404), calls=%async_computation.7 | async-start | bytes 1572864 | tf_op jit(solution)/shard_map/all_to_all | solution.py:134
  179.9 15.1 %all-to-all-start.6 = ((bf16[4,512,192]{1,2,0:T(8,128)(2,1)}), bf16[4,512,192]{1,2,0:T(8,128)(2,1)S(1)}, u32[]{:S(2)}, u32[]{:S(2)}) async-start(bf16[4,512,192]{1,2,0:T(8,128)(2,1)} %bitcast.405), calls=%async_computation.6 | async-start | bytes 1572864 | tf_op jit(solution)/shard_map/all_to_all | solution.py:136
  216.3 15.9 %all-to-all-start.9 = ((bf16[4,2,49152]{2,1,0:T(2,128)(2,1)}), bf16[4,2,49152]{2,1,0:T(2,128)(2,1)}, u32[]{:S(2)}, u32[]{:S(2)}) async-start(bf16[4,2,49152]{2,1,0:T(2,128)(2,1)} %reshape.509), calls=%async_computation.9 | async-start | bytes 1572864 | tf_op jit(solution)/shard_map/all_to_all | solution.py:157
  221.9 45.1 %copy-start.14 = (f32[4,24,8,512]{3,2,0,1:T(8,128)}, f32[4,24,8,512]{3,2,0,1:T(8,128)S(1)}, u32[]{:S(2)}) copy-start(f32[4,24,8,512]{3,2,0,1:T(8,128)S(1)} %copy.217) | copy-start | bytes 4718596
  292.8 15.9 %all-to-all-start.10 = ((bf16[4,512,192]{1,2,0:T(8,128)(2,1)}), bf16[4,512,192]{1,2,0:T(8,128)(2,1)}, u32[]{:S(2)}, u32[]{:S(2)}) async-start(bf16[4,512,192]{1,2,0:T(8,128)(2,1)} %bitcast.474), calls=%async_computation.10 | async-start | bytes 1572864 | tf_op jit(solution)/shard_map/all_to_all | solution.py:253
  339.1 26.0 %all-to-all-start.13 = ((bf16[4,2,49152]{2,1,0:T(2,128)(2,1)}), bf16[4,2,49152]{2,1,0:T(2,128)(2,1)S(1)}, u32[]{:S(2)}, u32[]{:S(2)}) async-start(bf16[4,2,49152]{2,1,0:T(2,128)(2,1)} %reshape.517), calls=%async_computation.13 | async-start | bytes 1572864 | tf_op jit(solution)/shard_map/all_to_all | solution.py:281
  365.1 28.2 %all-to-all-start.14 = ((bf16[4,2,49152]{2,1,0:T(2,128)(2,1)}), bf16[4,2,49152]{2,1,0:T(2,128)(2,1)}, u32[]{:S(2)}, u32[]{:S(2)}) async-start(bf16[4,2,49152]{2,1,0:T(2,128)(2,1)} %reshape.511), calls=%async_computation.14 | async-start | bytes 1572864 | tf_op jit(solution)/shard_map/all_to_all | solution.py:282
  393.3 18.5 %all-to-all-start.12 = ((bf16[4,2,49152]{2,1,0:T(2,128)(2,1)}), bf16[4,2,49152]{2,1,0:T(2,128)(2,1)}, u32[]{:S(2)}, u32[]{:S(2)}) async-start(bf16[4,2,49152]{2,1,0:T(2,128)(2,1)} %reshape.515), calls=%async_computation.12 | async-start | bytes 1572864 | tf_op jit(solution)/shard_map/all_to_all | solution.py:280
  411.8 22.0 %all-to-all-start.11 = ((bf16[4,2,49152]{2,1,0:T(2,128)(2,1)}), bf16[4,2,49152]{2,1,0:T(2,128)(2,1)}, u32[]{:S(2)}, u32[]{:S(2)}) async-start(bf16[4,2,49152]{2,1,0:T(2,128)(2,1)} %reshape.513), calls=%async_computation.11 | async-start | bytes 1572864 | tf_op jit(solution)/shard_map/all_to_all | solution.py:279
  463.8 16.3 %all-to-all-start.15 = ((bf16[4,512,192]{1,2,0:T(8,128)(2,1)}), bf16[4,512,192]{1,2,0:T(8,128)(2,1)}, u32[]{:S(2)}, u32[]{:S(2)}) async-start(bf16[4,512,192]{1,2,0:T(8,128)(2,1)} %bitcast.473), calls=%async_computation.15 | async-start | bytes 1572864 | tf_op jit(solution)/shard_map/all_to_all | solution.py:253
  512.8 29.3 %all-to-all-start.18 = ((bf16[4,2,49152]{2,1,0:T(2,128)(2,1)}), bf16[4,2,49152]{2,1,0:T(2,128)(2,1)}, u32[]{:S(2)}, u32[]{:S(2)}) async-start(bf16[4,2,49152]{2,1,0:T(2,128)(2,1)} %reshape.525), calls=%async_computation.18 | async-start | bytes 1572864 | tf_op jit(solution)/shard_map/all_to_all | solution.py:281
  542.1 25.9 %all-to-all-start.17 = ((bf16[4,2,49152]{2,1,0:T(2,128)(2,1)}), bf16[4,2,49152]{2,1,0:T(2,128)(2,1)}, u32[]{:S(2)}, u32[]{:S(2)}) async-start(bf16[4,2,49152]{2,1,0:T(2,128)(2,1)} %reshape.523), calls=%async_computation.17 | async-start | bytes 1572864 | tf_op jit(solution)/shard_map/all_to_all | solution.py:280
  546.3 160.1 %all-reduce.10.cloned.1.call-start = ((), (), s32[]{:S(2)}) async-start(), calls=%async_computation.20 | async-start | bytes 9437184 | tf_op jit(solution)/shard_map/psum | solution.py:384
  568.0 19.9 %all-to-all-start.16 = ((bf16[4,2,49152]{2,1,0:T(2,128)(2,1)}), bf16[4,2,49152]{2,1,0:T(2,128)(2,1)}, u32[]{:S(2)}, u32[]{:S(2)}) async-start(bf16[4,2,49152]{2,1,0:T(2,128)(2,1)} %reshape.521), calls=%async_computation.16 | async-start | bytes 1572864 | tf_op jit(solution)/shard_map/all_to_all | solution.py:279
  572.2 268.6 %all-reduce.12.cloned.1.call-start = ((), (), s32[]{:S(2)}) async-start(), calls=%async_computation.21 | async-start | bytes 6684672 | tf_op jit(solution)/shard_map/psum | solution.py:371
  610.0 51.5 %all-to-all-start.19 = ((bf16[4,2,49152]{2,1,0:T(2,128)(2,1)}), bf16[4,2,49152]{2,1,0:T(2,128)(2,1)}, u32[]{:S(2)}, u32[]{:S(2)}) async-start(bf16[4,2,49152]{2,1,0:T(2,128)(2,1)} %reshape.519), calls=%async_computation.19 | async-start | bytes 1572864 | tf_op jit(solution)/shard_map/all_to_all | solution.py:282
  (109 other events, 709.6 us)
Sparse Core Ops, SparseCore 0:
  553.3 147.5 all-reduce.9
  706.6 134.1 all-reduce.11
where the time goes:
time: 869 us; the launch traced here: 858 us
  waiting for transfers between devices  219 us (25%)
  matrix products  162 us (19%)
  local copies, waits for them, and re-layouts  131 us (15%)
  blocking collectives  127 us (15%)
  other arithmetic  121 us (14%)
  starting transfers between devices  81.2 us (9%)
  between operations  16.6 us (2%)
    psum x1, waiting for transfers between devices, shards(): lax.psum((stacked[0], stacked[1], stacked[6], stacked[7], stacked[8], sta...  134 us
    unnamed x270, local copies, waits for them, and re-layouts  76.3 us
    unnamed x11, other arithmetic  62.1 us
    psum x1, blocking collectives, shards(): lax.psum((stacked[2], stacked[3], stacked[4], stacked[5]), ('dp', 'grp'))  47.1 us
    psum x1, blocking collectives, shards(): lax.psum((stacked[0], stacked[1], stacked[6], stacked[7], stacked[8], sta...  37.8 us
    dot_general x2, matrix products, layer_forward(): jnp.dot(group_rows, widen_weight[layer_params, 0], preferred_element_type...  31.7 us
    psum x2, blocking collectives, layer_backward(): total_sum, total_cross = lax.psum((part_sum, part_cross), 'grp')  22.2 us
    sub x2, matrix products, single(): expon = jnp.exp(scores - highest)  21.1 us
  transfers between devices with their start and end apart: 22, of which 13 were waited for; matrix products, arithmetic and copies ran while one was open for 25% of the time, Pallas kernels for 0%

commit v1 on v0

--- a/solution.py
+++ b/solution.py
@@ -7,6 +7,29 @@
 HEAD = 64
 EPSILON = 1e-05
 MASKED = -1e30
+
+
+def split_up(x, dim, devices):
+    shape = x.shape
+    blocks = x.reshape(*shape[:dim], devices, shape[dim] // devices, *shape[dim + 1 :])
+    return jnp.moveaxis(blocks, dim, 0)
+
+
+def laid_out(pieces, dim):
+    pieces = jnp.moveaxis(pieces, 0, dim)
+    lengths = pieces.shape
+    return pieces.reshape(*lengths[:dim], lengths[dim] * lengths[dim + 1], *lengths[dim + 2 :])
+
+
+def swapped_with_each(value, axis, split_dim, concat_dim):
+    devices, index = (lax.axis_size(axis), lax.axis_index(axis))
+    pieces = split_up(value, split_dim, devices)
+    gathered = [pieces[index]]
+    for step in range(1, devices):
+        sent = pieces[index ^ step]
+        gathered.append(lax.ppermute(sent, axis, [(i, i ^ step) for i in range(devices)]))
+    pieces = jnp.stack(gathered)[index ^ jnp.arange(devices)]
+    return laid_out(pieces, concat_dim)
 
 
 def contract_rows(left, right):
@@ -250,9 +273,7 @@
     hidden_grad = (grad_after + contract_cols(widened_grad, widen_weight[layer_params, 0])).astype(
         jnp.bfloat16
     )
-    hidden_seq = lax.all_to_all(
-        hidden_grad.reshape(inputs.shape), "grp", split_axis=0, concat_axis=2, tiled=True
-    )
+    hidden_seq = swapped_with_each(hidden_grad.reshape(inputs.shape), "grp", 0, 2)
     seq_rows = hidden_seq.reshape(-1, width).astype(jnp.float32)
     first_gain_grad = jnp.sum(seq_rows * first_normed, axis=0)
     first_shift_grad = jnp.sum(seq_rows, axis=0)

time: 869 us -> 873 us (level)
  local copies, waits for them, and re-layouts: 131 us -> 146 us
    all_to_all x2 -> x0, waiting for transfers between devices: 15.4 us -> none  [layer_backward(): lax.all_to_all(hidden_grad.reshape(inputs.shape), 'grp', split_axis=0, co...]
    ppermute x0 -> x6, waiting for transfers between devices: none -> 11 us  [swapped_with_each(): lax.ppermute(sent, axis, [(i, i ^ step) for i in range(devices)])]
    all_to_all x2 -> x0, starting transfers between devices: 8.78 us -> none  [layer_backward(): lax.all_to_all(hidden_grad.reshape(inputs.shape), 'grp', split_axis=0, co...]
    unnamed x270 -> x280, local copies, waits for them, and re-layouts: 76.3 us -> 81.2 us
  transfers between devices with their start and end apart: 22 -> 26, of which waited for: 13 -> 15; matrix products, arithmetic and copies ran while one was open for 25% -> 25% of each run, Pallas kernels for 0% -> 0%
where the time goes in v1:
time: 873 us; the launch traced here: 863 us
  waiting for transfers between devices  214 us (25%)
  matrix products  161 us (18%)
  local copies, waits for them, and re-layouts  146 us (17%)
  blocking collectives  128 us (15%)
  other arithmetic  121 us (14%)
  starting transfers between devices  76.8 us (9%)
  between operations  16.7 us (2%)
    psum x1, waiting for transfers between devices, shards(): lax.psum((stacked[0], stacked[1], stacked[6], stacked[7], stacked[8], sta...  134 us
    unnamed x280, local copies, waits for them, and re-layouts  81.2 us
    unnamed x11, other arithmetic  63.2 us
    psum x1, blocking collectives, shards(): lax.psum((stacked[2], stacked[3], stacked[4], stacked[5]), ('dp', 'grp'))  47.4 us
    psum x1, blocking collectives, shards(): lax.psum((stacked[0], stacked[1], stacked[6], stacked[7], stacked[8], sta...  37.8 us
    dot_general x2, matrix products, layer_forward(): jnp.dot(group_rows, widen_weight[layer_params, 0], preferred_element_type...  31.7 us
    psum x2, blocking collectives, layer_backward(): total_sum, total_cross = lax.psum((part_sum, part_cross), 'grp')  22.4 us
    sub x2, matrix products, single(): expon = jnp.exp(scores - highest)  21.1 us
  transfers between devices with their start and end apart: 26, of which 15 were waited for; matrix products, arithmetic and copies ran while one was open for 25% of the time, Pallas kernels for 0%

profile of v1, /device:TPU:0, one launch (start us, length us, event | category | flops | bytes accessed | tf_op | source)
XLA Modules:
  0.0 862.6 jit_solution(10795794559348769253)
XLA Ops:
  31.4 6.9 all-to-all-done.3
  45.1 9.1 %all-to-all-done.2 = bf16[4,512,192]{1,2,0:T(8,128)(2,1)} async-done(((bf16[4,512,192]{1,2,0:T(8,128)(2,1)}), bf16[4,512,192]{1,2,0:T(8,128)(2,1)}, u32[]{:S(2)}, u32[]{:S(2)}) %all-to-all-start.2) | async-done | bytes 786464 | tf_op jit(solution)/shard_map/all_to_all | solution.py:157
  57.7 10.6 %fusion.130 = (f32[12,512]{1,0:T(8,128)S(1)}, f32[12,512,512]{1,2,0:T(8,128)}) fusion(pred[512]{0:T(512)(128)(4,1)S(1)} %iota_compare_fusion, bf16[512,12,64]{0,2,1:T(8,128)(2,1)} %bitcast.12, bf16[512,12,64]{0,2,1:T(8,128)(2,1)S(1)} %bitcast.469), kind=kOutput, calls=%fused_computation.300 | convolution fusion | flops 415236608 | bytes 14180864 | tf_op jit(solution)/shard_map/while/body/eval_jaxpr/sub | solution.py:65
  91.6 10.4 %all-to-all-done.4 = bf16[4,2,49152]{2,1,0:T(2,128)(2,1)S(1)} async-done(((bf16[4,2,49152]{2,1,0:T(2,128)(2,1)}), bf16[4,2,49152]{2,1,0:T(2,128)(2,1)S(1)}, u32[]{:S(2)}, u32[]{:S(2)}) %all-to-all-start.4) | async-done | bytes 786464 | tf_op jit(solution)/shard_map/all_to_all | solution.py:180
  103.8 15.9 %fusion.6 = (bf16[2048,768]{1,0:T(8,128)(2,1)S(1)}, f32[2048,768]{1,0:T(8,128)}) fusion(f32[768]{0:T(1024)S(1)} %get-tuple-element.241, bf16[2048,192]{0,1:T(8,128)(2,1)S(1)} %bitcast.527, bf16[2,1,192,768]{3,2,1,0:T(8,128)(2,1)S(1)} %copy-done.67), kind=kOutput, calls=%fused_computation.20 | convolution fusion | flops 707788800 | bytes 10522624 | tf_op jit(solution)/shard_map/dot_general | solution.py:183
  121.4 10.1 %all-reduce.6 = (f32[2048]{0:T(1024)S(1)}, f32[2048]{0:T(1024)S(1)}) all-reduce(f32[2048]{0:T(1024)S(1)} %get-tuple-element.233, f32[2048]{0:T(1024)S(1)} %get-tuple-element.232), channel_id=1, replica_groups=mesh['dp'=8,'grp'=4] {'grp'}, use_global_device_ids=true, to_apply=%region_7.8 | all-reduce | flops 4096 | bytes 32768 | tf_op jit(solution)/shard_map/psum | solution.py:194
  155.4 8.5 all-to-all-done.8
  171.0 8.9 %all-to-all-done.7 = bf16[4,512,192]{1,2,0:T(8,128)(2,1)} async-done(((bf16[4,512,192]{1,2,0:T(8,128)(2,1)}), bf16[4,512,192]{1,2,0:T(8,128)(2,1)}, u32[]{:S(2)}, u32[]{:S(2)}) %all-to-all-start.7) | async-done | bytes 786464 | tf_op jit(solution)/shard_map/all_to_all | solution.py:157
  183.4 10.5 %fusion.132 = (f32[12,512]{1,0:T(8,128)S(1)}, f32[12,512,512]{1,2,0:T(8,128)}) fusion(pred[512]{0:T(512)(128)(4,1)S(1)} %iota_compare_fusion, bf16[512,12,64]{0,2,1:T(8,128)(2,1)} %bitcast.37, bf16[512,12,64]{0,2,1:T(8,128)(2,1)S(1)} %bitcast.471), kind=kOutput, calls=%fused_computation.302 | convolution fusion | flops 415236608 | bytes 14180864 | tf_op jit(solution)/shard_map/while/body/eval_jaxpr/sub | solution.py:65
  222.6 9.6 %all-to-all-done.9 = bf16[4,2,49152]{2,1,0:T(2,128)(2,1)} async-done(((bf16[4,2,49152]{2,1,0:T(2,128)(2,1)}), bf16[4,2,49152]{2,1,0:T(2,128)(2,1)}, u32[]{:S(2)}, u32[]{:S(2)}) %all-to-all-start.9) | async-done | bytes 786464 | tf_op jit(solution)/shard_map/all_to_all | solution.py:180
  238.5 15.9 %fusion.9 = (bf16[2048,768]{1,0:T(8,128)(2,1)S(1)}, f32[2048,768]{1,0:T(8,128)}) fusion(f32[768]{0:T(1024)S(1)} %get-tuple-element.240, bf16[2048,192]{0,1:T(8,128)(2,1)S(1)} %bitcast.531, bf16[2,1,192,768]{3,2,1,0:T(8,128)(2,1)S(1)} %copy-done.68), kind=kOutput, calls=%fused_computation.23 | convolution fusion | flops 707788800 | bytes 10522624 | tf_op jit(solution)/shard_map/dot_general | solution.py:183
  256.7 10.3 %all-reduce.5 = (f32[2048]{0:T(1024)S(1)}, f32[2048]{0:T(1024)S(1)}) all-reduce(f32[2048]{0:T(1024)S(1)} %get-tuple-element.231, f32[2048]{0:T(1024)S(1)} %get-tuple-element.230), channel_id=1, replica_groups=mesh['dp'=8,'grp'=4] {'grp'}, use_global_device_ids=true, to_apply=%region_15.16 | all-reduce | flops 4096 | bytes 32768 | tf_op jit(solution)/shard_map/psum | solution.py:194
  269.4 10.1 %all-reduce.4 = (f32[2048]{0:T(1024)S(1)}, f32[2048]{0:T(1024)S(1)}) all-reduce(f32[2048]{0:T(1024)S(1)} %get-tuple-element.223, f32[2048]{0:T(1024)S(1)} %bitcast.569), channel_id=1, replica_groups=mesh['dp'=8,'grp'=4] {'grp'}, use_global_device_ids=true, to_apply=%region_19.20 | all-reduce | flops 4096 | bytes 32768 | tf_op jit(solution)/shard_map/psum | solution.py:260
  326.6 6.9 fusion.70
  347.1 11.6 %multiply_reduce_fusion.1 = (f32[12,512]{1,0:T(8,128)S(1)}, f32[12,512,512]{1,2,0:T(8,128)}) fusion(f32[12,512,512]{1,2,0:T(8,128)} %get-tuple-element.310, f32[12,512]{1,0:T(8,128)S(1)} %get-tuple-element.309, bf16[512,12,64]{0,2,1:T(8,128)(2,1)} %bitcast.547, bf16[512,12,64]{0,2,1:T(8,128)(2,1)} %bitcast.544), kind=kOutput, calls=%fused_computation.7 | convolution fusion | flops 412084224 | bytes 26787840 | tf_op jit(solution)/shard_map/while/body/eval_jaxpr/qhd,khd->hqk/dot_general | solution.py:84
  374.0 9.6 %multiply_convert_fusion.1 = bf16[12,512,512]{1,2,0:T(8,128)(2,1)S(1)} fusion(f32[12,512,512]{1,2,0:T(8,128)} %get-tuple-element.317, f32[12,512]{1,0:T(8,128)S(1)} %get-tuple-element.316, f32[12,512,512]{1,2,0:T(8,128)} %get-tuple-element.310, f32[12,512]{1,0:T(8,128)S(1)} %get-tuple-element.309), kind=kLoop, calls=%fused_computation.6 | loop fusion | flops 12582912 | bytes 31506432 | tf_op jit(solution)/shard_map/while/body/eval_jaxpr/convert_element_type | solution.py:88
  411.5 7.5 reduce.31
  452.4 12.3 %all-reduce.3 = (f32[2048]{0:T(1024)S(1)}, f32[2048]{0:T(1024)S(1)}) all-reduce(f32[2048]{0:T(1024)S(1)} %get-tuple-element.221, f32[2048]{0:T(1024)S(1)} %get-tuple-element.228), channel_id=1, replica_groups=mesh['dp'=8,'grp'=4] {'grp'}, use_global_device_ids=true, to_apply=%region_26.27 | all-reduce | flops 4096 | bytes 32768 | tf_op jit(solution)/shard_map/psum | solution.py:260
  500.5 8.9 %multiply_reduce_fusion = (f32[12,512]{1,0:T(8,128)S(1)}, f32[12,512,512]{1,2,0:T(8,128)}) fusion(f32[12,512,512]{1,2,0:T(8,128)} %get-tuple-element.303, f32[12,512]{1,0:T(8,128)S(1)} %copy-done.82, bf16[512,12,64]{0,2,1:T(8,128)(2,1)S(1)} %bitcast.549, bf16[512,12,64]{0,2,1:T(8,128)(2,1)S(1)} %bitcast.542), kind=kOutput, calls=%fused_computation.5 | convolution fusion | flops 412084224 | bytes 26787840 | tf_op jit(solution)/shard_map/while/body/eval_jaxpr/qhd,khd->hqk/dot_general | solution.py:84
  521.8 9.6 %multiply_convert_fusion = bf16[12,512,512]{1,2,0:T(8,128)(2,1)S(1)} fusion(f32[12,512,512]{1,2,0:T(8,128)} %get-tuple-element.320, f32[12,512]{1,0:T(8,128)S(1)} %get-tuple-element.319, f32[12,512,512]{1,2,0:T(8,128)} %get-tuple-element.303, f32[12,512]{1,0:T(8,128)S(1)} %copy-done.82), kind=kLoop, calls=%fused_computation.4 | loop fusion | flops 12582912 | bytes 31506432 | tf_op jit(solution)/shard_map/while/body/eval_jaxpr/convert_element_type | solution.py:88
  562.8 7.5 reduce.35
  619.1 47.4 %all-reduce = (f32[2,768]{1,0:T(2,128)}, f32[2,768]{1,0:T(2,128)}, f32[2,768]{1,0:T(2,128)}) all-reduce(f32[2,768]{1,0:T(2,128)S(1)} %pad_maximum_fusion.4, f32[2,768]{1,0:T(2,128)S(1)} %pad_maximum_fusion.5, f32[2,768]{1,0:T(2,128)S(1)} %pad_maximum_fusion.6), channel_id=1, replica_groups=mesh['dp'=8,'grp'=4] {'dp','grp'}, use_global_device_ids=true, to_apply=%region_39.40 | all-reduce | flops 4608 | bytes 36864 | tf_op jit(solution)/shard_map/psum | solution.py:405
  673.6 37.8 %all-reduce.1 = (f32[2,2,192]{2,1,0:T(2,128)}, f32[2,768]{1,0:T(2,128)}, f32[2,192]{1,0:T(2,128)}, f32[2,192]{1,0:T(2,128)}, f32[2,192]{1,0:T(2,128)}) all-reduce(f32[2,2,192]{2,1,0:T(2,128)S(1)} %pad_maximum_fusion.8, f32[2,768]{1,0:T(2,128)S(1)} %pad_maximum_fusion.7, ...), channel_id=1, replica_groups=mesh['dp'=8,'grp'=4] {'dp'}, use_global_device_ids=true, to_apply=%region_35.36 | all-reduce | flops 3456 | bytes 27648 | tf_op jit(solution)/shard_map/psum | solution.py:392
  711.4 134.1 %all-reduce.12.cloned.1.call-done = (f32[2,1,192,576]{3,2,1,0:T(8,128)}, f32[2,1,192,768]{3,2,1,0:T(8,128)}, f32[2,1,768,192]{2,3,1,0:T(8,128)}) async-done(((f32[2,1,192,576]{3,2,1,0:T(8,128)}, f32[2,1,192,768]{3,2,1,0:T(8,128)}, f32[2,1,768,192]{2,3,1,0:T(8,128)}), (f32[2,1,192,576]{3,2,1,0:T(8,128)}, f32[2,1,192,768]{3,2,1,0:T(8,128)}, f32[2,1,768,192]{2,3,1,0:T(8,128)})) %all-reduce.12.cloned.1.call-update) | async-done | bytes 3244048 | tf_op jit(solution)/shard_map/psum | solution.py:392
  (492 shorter events, 415.9 us)
Async XLA Ops:
  7.2 16.0 %all-to-all-start = ((bf16[4,512,192]{1,2,0:T(8,128)(2,1)}), bf16[4,512,192]{1,2,0:T(8,128)(2,1)S(1)}, u32[]{:S(2)}, u32[]{:S(2)}) async-start(bf16[4,512,192]{1,2,0:T(8,128)(2,1)} %param.15), calls=%async_computation | async-start | bytes 1572864 | tf_op jit(solution)/shard_map/all_to_all | solution.py:160
  23.2 15.1 %all-to-all-start.3 = ((bf16[4,512,192]{1,2,0:T(8,128)(2,1)}), bf16[4,512,192]{1,2,0:T(8,128)(2,1)S(1)}, u32[]{:S(2)}, u32[]{:S(2)}) async-start(bf16[4,512,192]{1,2,0:T(8,128)(2,1)} %bitcast.439), calls=%async_computation.3 | async-start | bytes 1572864 | tf_op jit(solution)/shard_map/all_to_all | solution.py:158
  38.3 15.9 %all-to-all-start.2 = ((bf16[4,512,192]{1,2,0:T(8,128)(2,1)}), bf16[4,512,192]{1,2,0:T(8,128)(2,1)}, u32[]{:S(2)}, u32[]{:S(2)}) async-start(bf16[4,512,192]{1,2,0:T(8,128)(2,1)} %bitcast.440), calls=%async_computation.2 | async-start | bytes 1572864 | tf_op jit(solution)/shard_map/all_to_all | solution.py:157
  54.2 15.1 %all-to-all-start.1 = ((bf16[4,512,192]{1,2,0:T(8,128)(2,1)}), bf16[4,512,192]{1,2,0:T(8,128)(2,1)S(1)}, u32[]{:S(2)}, u32[]{:S(2)}) async-start(bf16[4,512,192]{1,2,0:T(8,128)(2,1)} %bitcast.441), calls=%async_computation.1 | async-start | bytes 1572864 | tf_op jit(solution)/shard_map/all_to_all | solution.py:159
  86.8 15.1 %all-to-all-start.4 = ((bf16[4,2,49152]{2,1,0:T(2,128)(2,1)}), bf16[4,2,49152]{2,1,0:T(2,128)(2,1)S(1)}, u32[]{:S(2)}, u32[]{:S(2)}) async-start(bf16[4,2,49152]{2,1,0:T(2,128)(2,1)} %reshape.523), calls=%async_computation.4 | async-start | bytes 1572864 | tf_op jit(solution)/shard_map/all_to_all | solution.py:180
  133.5 15.1 %all-to-all-start.5 = ((bf16[4,512,192]{1,2,0:T(8,128)(2,1)}), bf16[4,512,192]{1,2,0:T(8,128)(2,1)S(1)}, u32[]{:S(2)}, u32[]{:S(2)}) async-start(bf16[4,512,192]{1,2,0:T(8,128)(2,1)} %bitcast.438), calls=%async_computation.5 | async-start | bytes 1572864 | tf_op jit(solution)/shard_map/all_to_all | solution.py:160
  148.6 15.3 %all-to-all-start.8 = ((bf16[4,512,192]{1,2,0:T(8,128)(2,1)}), bf16[4,512,192]{1,2,0:T(8,128)(2,1)S(1)}, u32[]{:S(2)}, u32[]{:S(2)}) async-start(bf16[4,512,192]{1,2,0:T(8,128)(2,1)} %bitcast.435), calls=%async_computation.8 | async-start | bytes 1572864 | tf_op jit(solution)/shard_map/all_to_all | solution.py:158
  164.0 15.9 %all-to-all-start.7 = ((bf16[4,512,192]{1,2,0:T(8,128)(2,1)}), bf16[4,512,192]{1,2,0:T(8,128)(2,1)}, u32[]{:S(2)}, u32[]{:S(2)}) async-start(bf16[4,512,192]{1,2,0:T(8,128)(2,1)} %bitcast.436), calls=%async_computation.7 | async-start | bytes 1572864 | tf_op jit(solution)/shard_map/all_to_all | solution.py:157
  179.9 15.1 %all-to-all-start.6 = ((bf16[4,512,192]{1,2,0:T(8,128)(2,1)}), bf16[4,512,192]{1,2,0:T(8,128)(2,1)S(1)}, u32[]{:S(2)}, u32[]{:S(2)}) async-start(bf16[4,512,192]{1,2,0:T(8,128)(2,1)} %bitcast.437), calls=%async_computation.6 | async-start | bytes 1572864 | tf_op jit(solution)/shard_map/all_to_all | solution.py:159
  216.3 15.9 %all-to-all-start.9 = ((bf16[4,2,49152]{2,1,0:T(2,128)(2,1)}), bf16[4,2,49152]{2,1,0:T(2,128)(2,1)}, u32[]{:S(2)}, u32[]{:S(2)}) async-start(bf16[4,2,49152]{2,1,0:T(2,128)(2,1)} %reshape.525), calls=%async_computation.9 | async-start | bytes 1572864 | tf_op jit(solution)/shard_map/all_to_all | solution.py:180
  300.8 7.6 collective-permute-start.1
  302.0 7.4 collective-permute-start.2
  302.0 7.4 collective-permute-start
  343.6 25.8 %all-to-all-start.12 = ((bf16[4,2,49152]{2,1,0:T(2,128)(2,1)}), bf16[4,2,49152]{2,1,0:T(2,128)(2,1)S(1)}, u32[]{:S(2)}, u32[]{:S(2)}) async-start(bf16[4,2,49152]{2,1,0:T(2,128)(2,1)} %reshape.533), calls=%async_computation.12 | async-start | bytes 1572864 | tf_op jit(solution)/shard_map/all_to_all | solution.py:302
  369.3 27.9 %all-to-all-start.13 = ((bf16[4,2,49152]{2,1,0:T(2,128)(2,1)}), bf16[4,2,49152]{2,1,0:T(2,128)(2,1)}, u32[]{:S(2)}, u32[]{:S(2)}) async-start(bf16[4,2,49152]{2,1,0:T(2,128)(2,1)} %reshape.527), calls=%async_computation.13 | async-start | bytes 1572864 | tf_op jit(solution)/shard_map/all_to_all | solution.py:303
  397.2 24.1 %all-to-all-start.11 = ((bf16[4,2,49152]{2,1,0:T(2,128)(2,1)}), bf16[4,2,49152]{2,1,0:T(2,128)(2,1)}, u32[]{:S(2)}, u32[]{:S(2)}) async-start(bf16[4,2,49152]{2,1,0:T(2,128)(2,1)} %reshape.531), calls=%async_computation.11 | async-start | bytes 1572864 | tf_op jit(solution)/shard_map/all_to_all | solution.py:301
  421.3 23.0 %all-to-all-start.10 = ((bf16[4,2,49152]{2,1,0:T(2,128)(2,1)}), bf16[4,2,49152]{2,1,0:T(2,128)(2,1)}, u32[]{:S(2)}, u32[]{:S(2)}) async-start(bf16[4,2,49152]{2,1,0:T(2,128)(2,1)} %reshape.529), calls=%async_computation.10 | async-start | bytes 1572864 | tf_op jit(solution)/shard_map/all_to_all | solution.py:300
  477.7 7.5 collective-permute-start.4
  517.5 29.3 %all-to-all-start.16 = ((bf16[4,2,49152]{2,1,0:T(2,128)(2,1)}), bf16[4,2,49152]{2,1,0:T(2,128)(2,1)}, u32[]{:S(2)}, u32[]{:S(2)}) async-start(bf16[4,2,49152]{2,1,0:T(2,128)(2,1)} %reshape.541), calls=%async_computation.16 | async-start | bytes 1572864 | tf_op jit(solution)/shard_map/all_to_all | solution.py:302
  546.8 25.9 %all-to-all-start.15 = ((bf16[4,2,49152]{2,1,0:T(2,128)(2,1)}), bf16[4,2,49152]{2,1,0:T(2,128)(2,1)}, u32[]{:S(2)}, u32[]{:S(2)}) async-start(bf16[4,2,49152]{2,1,0:T(2,128)(2,1)} %reshape.539), calls=%async_computation.15 | async-start | bytes 1572864 | tf_op jit(solution)/shard_map/all_to_all | solution.py:301
  551.0 160.4 %all-reduce.10.cloned.1.call-start = ((), (), s32[]{:S(2)}) async-start(), calls=%async_computation.18 | async-start | bytes 9437184 | tf_op jit(solution)/shard_map/psum | solution.py:405
  572.6 19.9 %all-to-all-start.14 = ((bf16[4,2,49152]{2,1,0:T(2,128)(2,1)}), bf16[4,2,49152]{2,1,0:T(2,128)(2,1)}, u32[]{:S(2)}, u32[]{:S(2)}) async-start(bf16[4,2,49152]{2,1,0:T(2,128)(2,1)} %reshape.537), calls=%async_computation.14 | async-start | bytes 1572864 | tf_op jit(solution)/shard_map/all_to_all | solution.py:300
  576.8 268.6 %all-reduce.12.cloned.1.call-start = ((), (), s32[]{:S(2)}) async-start(), calls=%async_computation.19 | async-start | bytes 6684672 | tf_op jit(solution)/shard_map/psum | solution.py:392
  614.7 51.8 %all-to-all-start.17 = ((bf16[4,2,49152]{2,1,0:T(2,128)(2,1)}), bf16[4,2,49152]{2,1,0:T(2,128)(2,1)}, u32[]{:S(2)}, u32[]{:S(2)}) async-start(bf16[4,2,49152]{2,1,0:T(2,128)(2,1)} %reshape.535), calls=%async_computation.17 | async-start | bytes 1572864 | tf_op jit(solution)/shard_map/all_to_all | solution.py:303
  (114 other events, 924.1 us)
Sparse Core Ops, SparseCore 0:
  558.0 147.8 all-reduce.9
  711.5 133.8 all-reduce.11
